TPU v7x, 32 devices: a whole 2x2x4 slice. The times are simulated.
32 devices in a mesh: row: 8 (over y, x, core), col: 4 (over z).
Axes of the slice: x: 2, y: 2, z: 4, core: 2. Of those that a mesh axis runs over, the one named last changes fastest.
Arguments:
- alpha_prev: float32 [48, 4096], P(None, 'row'), may hold values from 0.1 to 10
- tokens: int32 [48], replicated, may hold values from 0 to 16639
- src_emb: bfloat16 [4096, 256], P('row'), may hold values from -10 to 10
- dst_emb: bfloat16 [256, 4096], P(None, ('row', 'col')), may hold values from -7 to 7
- emission: bfloat16 [16640, 4096], P(None, ('row', 'col')), may hold values from 0.02 to 8, as said below
Outputs:
- next_alpha: float32 [48, 4096], P(None, 'row')
- log_total: float32 [48], replicated
Inputs may be any that keep to these rules, and one draw needn't show every extreme that they name: `emission`: every weight is positive.
All inputs are finite; a program needn't handle non-finite values.
Results may differ from a plain program's by a relative error of at most 0.0014.
Values may be sent and summed in bfloat16 or wider, within the bound.
No kernel may reach another device: no remote copies, remote signals or barrier semaphores. Data moves between devices by JAX's collectives and lax.ppermute only.
A program may use at most 128 MiB of HBM per device.

v0:
```python
import math
import jax
import jax.numpy as jnp
from jax import lax
from jax.sharding import PartitionSpec as P


def absorb(folded, sources, shard_piece, group_cols):
    src_rows = sources.shape[0]
    piece_groups = shard_piece.shape[1] // group_cols
    per_turn = math.gcd(piece_groups, max(1, (1 << 20) // (src_rows * group_cols)))

    def absorb_block(turn_index, tile_state):
        expo_tile, part_peak, part_total = tile_state
        offset = turn_index * (per_turn * group_cols)
        columns = lax.dynamic_slice_in_dim(shard_piece, offset, per_turn * group_cols, 1)
        logits = jnp.dot(sources, columns, preferred_element_type=jnp.float32).reshape(
            src_rows, per_turn, group_cols
        )
        block_peak = jnp.max(logits, axis=2)
        shifted = jnp.exp(logits - block_peak[:, :, None])
        block_total = jnp.sum(shifted, axis=2)
        expo_block = shifted.reshape(src_rows, per_turn * group_cols).astype(jnp.bfloat16)
        expo_tile = lax.dynamic_update_slice_in_dim(expo_tile, expo_block, offset, 1)
        group_slot = turn_index * per_turn
        part_peak = lax.dynamic_update_slice_in_dim(part_peak, block_peak, group_slot, 1)
        part_total = lax.dynamic_update_slice_in_dim(part_total, block_total, group_slot, 1)
        return (expo_tile, part_peak, part_total)

    return lax.fori_loop(0, piece_groups // per_turn, absorb_block, folded)


def start_state(src_rows, tile_cols, group_cols):
    groups = tile_cols // group_cols
    return (
        jnp.zeros((src_rows, tile_cols), jnp.bfloat16),
        jnp.zeros((src_rows, groups), jnp.float32),
        jnp.zeros((src_rows, groups), jnp.float32),
    )


def on_device(alpha_prev, tokens, src_emb, dst_emb, emission):
    group_cols = dst_emb.shape[1]
    row_count = lax.axis_size("row")
    col_count = lax.axis_size("col")
    seq_count = alpha_prev.shape[0]
    row_index = lax.axis_index("row")
    tile_cols = group_cols * row_count
    folded = absorb(
        start_state(src_emb.shape[0], tile_cols, group_cols),
        src_emb,
        lax.all_gather(dst_emb, "row", axis=1, tiled=True),
        group_cols,
    )
    expo_tile, part_peak, part_total = folded
    src_rows = src_emb.shape[0]
    local_peak = jnp.max(part_peak, axis=1)
    local_total = jnp.sum(part_total * jnp.exp(part_peak - local_peak[:, None]), axis=1)
    row_peak = lax.pmax(local_peak, "col")
    row_total = lax.psum(local_total * jnp.exp(local_peak - row_peak), "col")
    row_scale = jnp.exp(part_peak - row_peak[:, None]) / row_total[:, None]
    local_groups = tile_cols // group_cols
    per_block = math.gcd(local_groups, 16)

    def multiply(block_index, partial_value):
        group_start = block_index * per_block
        scale_cols = lax.dynamic_slice_in_dim(row_scale, group_start, per_block, 1)
        weights = (scale_cols.T[:, None, :] * alpha_prev[None, :, :]).astype(jnp.bfloat16)
        expo_cols = lax.dynamic_slice_in_dim(
            expo_tile, group_start * group_cols, per_block * group_cols, 1
        ).reshape(src_rows, per_block, group_cols)
        product = jnp.einsum("gbi,igk->bgk", weights, expo_cols, preferred_element_type=jnp.float32)
        return lax.dynamic_update_slice_in_dim(
            partial_value,
            product.reshape(seq_count, per_block * group_cols),
            group_start * group_cols,
            1,
        )

    partial_value = lax.fori_loop(
        0, local_groups // per_block, multiply, jnp.zeros((seq_count, tile_cols), jnp.float32)
    )
    summed = lax.psum(partial_value, "row")
    own_sums = lax.dynamic_slice_in_dim(summed, row_index * group_cols, group_cols, 1)
    emit_rows = jnp.take(emission, tokens, axis=0).astype(jnp.float32)
    emitted = own_sums * emit_rows
    state_count = float(group_cols * row_count * col_count)
    total = lax.psum(jnp.sum(emitted, axis=1), ("row", "col"))
    scaled = emitted * (state_count / total)[:, None]
    next_alpha = lax.all_gather(scaled, "col", axis=1, tiled=True)
    log_total = jnp.log(total)
    return (next_alpha, log_total)


def solution(mesh):
    placed = (P(None, "row"), P(), P("row", None), P(None, ("row", "col")), P(None, ("row", "col")))
    return jax.shard_map(
        on_device, mesh=mesh, in_specs=placed, out_specs=(P(None, "row"), P()), check_vma=False
    )
```

profile of v0, /device:TPU:0, one launch (start us, length us, event | category | flops | bytes accessed | tf_op | source)
XLA Modules:
  0.0 166.4 jit_solution(14309806764282524219)
XLA Ops:
  7.2 0.0 copy-start
  7.2 0.0 all-reduce.2.cloned.1.call-start
  7.2 11.9 %all_gather.6 = bf16[256,1024]{1,0:T(8,128)(2,1)S(1)} all-gather(bf16[256,128]{1,0:T(8,128)(2,1)} %param.8), channel_id=1, replica_groups=mesh['row'=8,'col'=4] {'row'}, dimensions={1}, use_global_device_ids=true | all-gather | bytes 589824 | tf_op jit(solution)/shard_map/all_gather | solution.py:52
  19.1 0.0 copy-done
  19.1 0.4 fusion.11
  19.5 1.8 %copy.20 = f32[64,8,8,128]{3,2,1,0:T(8,128)} copy(f32[64,8,8,128]{3,1,2,0:T(8,128)S(1)} %bitcast.26) | data formatting | bytes 4194304
  21.3 2.2 %reduce_max.19 = f32[512,8]{1,0:T(8,128)S(1)} reduce(f32[512,8,128]{2,1,0:T(8,128)} %bitcast.27, f32[]{:T(128)} %constant.29.clone.1), dimensions={2}, to_apply=%region_0.1 | reduce | flops 520192 | bytes 2113540 | tf_op jit(solution)/shard_map/while/body/eval_jaxpr/reduce_max | solution.py:20
  23.6 2.8 %exponential_reduce_fusion = f32[512,8]{1,0:T(8,128)S(1)} fusion(f32[512,8,128]{2,1,0:T(8,128)} %bitcast.28, f32[512,8]{1,0:T(8,128)S(1)} %reduce_max.19), kind=kLoop, calls=%fused_computation.4 | loop fusion | flops 1044480 | bytes 2129920 | tf_op jit(solution)/shard_map/while/body/eval_jaxpr/reduce_sum | solution.py:22
  26.4 0.1 copy.15
  26.5 0.6 sub.38
  27.1 0.0 copy-start.1
  27.1 1.5 fusion.9
  28.6 0.0 copy-start.2
  28.6 12.1 %pmax.7 = f32[512]{0:T(512)S(1)} all-reduce(f32[512]{0:T(512)S(1)} %get-tuple-element.29), channel_id=1, replica_groups=mesh['row'=8,'col'=4] {'col'}, use_global_device_ids=true, to_apply=%region_2.3 | all-reduce | flops 512 | bytes 4096 | tf_op jit(solution)/shard_map/pmax | solution.py:59
  40.7 0.2 multiply_reduce_fusion
  41.0 8.4 %psum.21 = f32[512]{0:T(512)S(1)} all-reduce(f32[512]{0:T(512)S(1)} %exponential_multiply_fusion), channel_id=1, replica_groups=mesh['row'=8,'col'=4] {'col'}, use_global_device_ids=true, to_apply=%region_5.0 | all-reduce | flops 512 | bytes 4096 | tf_op jit(solution)/shard_map/psum | solution.py:60
  49.4 0.0 copy-done.1
  49.4 1.6 convolution_bitcast_fusion
  51.0 0.7 copy.30
  51.7 0.0 all-reduce.2.cloned.1.call-update
  51.7 0.0 copy-done.2
  51.8 3.3 %gather_fusion = bf16[48,128]{1,0:T(8,128)(2,1)S(1)} fusion(bf16[16640,128]{1,0:T(8,128)(2,1)} %param.9, s32[1024]{0:T(1024)S(1)} %pad_clamp_fusion), kind=kCustom, calls=%fused_computation | custom fusion | bytes 24768 | tf_op jit(solution)/shard_map/jit(_take)/gather | solution.py:85
  55.1 48.8 %all-reduce.2.cloned.1.call-done = f32[48,1024]{1,0:T(8,128)} async-done(((f32[48,1024]{1,0:T(8,128)}), f32[48,1024]{1,0:T(8,128)}) %all-reduce.2.cloned.1.call-update) | async-done | bytes 196624 | tf_op jit(solution)/shard_map/psum | solution.py:83
  103.9 0.9 fusion.8
  104.8 39.3 %psum.23 = f32[48]{0:T(128)S(1)} all-reduce(f32[48]{0:T(128)S(1)} %fusion.8), channel_id=1, replica_groups=mesh['row'=8,'col'=4] {'row','col'}, use_global_device_ids=true, to_apply=%region_8.0 | all-reduce | flops 48 | bytes 384 | tf_op jit(solution)/shard_map/psum | solution.py:88
  144.2 0.5 fusion.10
  144.7 0.8 fusion.7
  145.5 13.3 %all_gather.7 = f32[48,512]{1,0:T(8,128)S(1)} all-gather(f32[48,128]{1,0:T(8,128)S(1)} %fusion.7), channel_id=1, replica_groups=mesh['row'=8,'col'=4] {'col'}, dimensions={1}, use_global_device_ids=true | all-gather | bytes 122880 | tf_op jit(solution)/shard_map/all_gather | solution.py:90
  158.9 0.6 copy.33
  (5 shorter events, 0.0 us)
Async XLA Ops:
  7.2 11.9 %copy-start = (bf16[512,256]{1,0:T(8,128)(2,1)S(1)}, bf16[512,256]{1,0:T(8,128)(2,1)}, u32[]{:S(2)}) copy-start(bf16[512,256]{1,0:T(8,128)(2,1)} %param.7) | copy-start | bytes 786436
  7.2 96.7 %all-reduce.2.cloned.1.call-start = ((), (), s32[]{:S(2)}) async-start(), calls=%async_computation | async-start | bytes 393216 | tf_op jit(solution)/shard_map/psum | solution.py:83
  27.1 22.3 %copy-start.1 = (f32[48,512]{1,0:T(8,128)S(1)}, f32[48,512]{1,0:T(8,128)}, u32[]{:S(2)}) copy-start(f32[48,512]{1,0:T(8,128)} %param.5) | copy-start | bytes 294916
  28.6 23.1 %copy-start.2 = (s32[48]{0:T(128)S(1)}, s32[48]{0:T(128)}, u32[]{:S(2)}) copy-start(s32[48]{0:T(128)} %param.6) | copy-start | bytes 580
Sparse Core Ops, SparseCore 0:
  51.8 52.0 all-reduce.1
where the time goes:
time: 167 us; the launch traced here: 166 us
  blocking collectives  85 us (51%)
  waiting for transfers between devices  48.8 us (29%)
  between operations  14.1 us (8%)
  other arithmetic  9.08 us (5%)
  local copies, waits for them, and re-layouts  7.22 us (4%)
  matrix products  2.06 us (1%)
    psum x1, waiting for transfers between devices, on_device(): summed = lax.psum(partial_value, 'row')  48.8 us
    psum x1, blocking collectives, on_device(): total = lax.psum(jnp.sum(emitted, axis=1), ('row', 'col'))  39.3 us
    all_gather x1, blocking collectives, on_device(): next_alpha = lax.all_gather(scaled, 'col', axis=1, tiled=True)  13.3 us
    pmax x1, blocking collectives, on_device(): row_peak = lax.pmax(local_peak, 'col')  12.1 us
    all_gather x1, blocking collectives, on_device(): lax.all_gather(dst_emb, 'row', axis=1, tiled=True)  11.9 us
    psum x1, blocking collectives, on_device(): row_total = lax.psum(local_total * jnp.exp(local_peak - row_peak), 'col')  8.37 us
    gather x1, local copies, waits for them, and re-layouts, on_device(): emit_rows = jnp.take(emission, tokens, axis=0).astype(jnp.float32)  3.35 us
  transfers between devices with their start and end apart: 1, of which 1 were waited for; matrix products, arithmetic and copies ran while one was open for 2% of the time, Pallas kernels for 0%

commit v1 on v0

--- a/solution.py
+++ b/solution.py
@@ -80,7 +80,8 @@
     partial_value = lax.fori_loop(
         0, local_groups // per_block, multiply, jnp.zeros((seq_count, tile_cols), jnp.float32)
     )
-    summed = lax.psum(partial_value, "row")
+    parts = lax.all_gather(partial_value, "row")
+    summed = jnp.sum(parts, axis=0)
     own_sums = lax.dynamic_slice_in_dim(summed, row_index * group_cols, group_cols, 1)
     emit_rows = jnp.take(emission, tokens, axis=0).astype(jnp.float32)
     emitted = own_sums * emit_rows

time: 167 us -> 139 us (0.83)
  waiting for transfers between devices: 48.8 us -> 21.1 us
    psum x1 -> x0, waiting for transfers between devices: 48.8 us -> none  [on_device(): summed = lax.psum(partial_value, 'row')]
    all_gather x0 -> x1, waiting for transfers between devices: none -> 21.1 us  [on_device(): parts = lax.all_gather(partial_value, 'row')]
where the time goes in v1:
time: 139 us
  blocking collectives  85 us (61%)
  waiting for transfers between devices  21.1 us (15%)
  between operations  14.1 us (10%)
  other arithmetic  9.13 us (7%)
  local copies, waits for them, and re-layouts  7.3 us (5%)
  matrix products  2.06 us (1%)
    psum x1, blocking collectives, on_device(): total = lax.psum(jnp.sum(emitted, axis=1), ('row', 'col'))  39.3 us
    all_gather x1, waiting for transfers between devices, on_device(): parts = lax.all_gather(partial_value, 'row')  21.1 us
    all_gather x1, blocking collectives, on_device(): next_alpha = lax.all_gather(scaled, 'col', axis=1, tiled=True)  13.3 us
    pmax x1, blocking collectives, on_device(): row_peak = lax.pmax(local_peak, 'col')  12.1 us
    all_gather x1, blocking collectives, on_device(): lax.all_gather(dst_emb, 'row', axis=1, tiled=True)  11.9 us
    psum x1, blocking collectives, on_device(): row_total = lax.psum(local_total * jnp.exp(local_peak - row_peak), 'col')  8.37 us
    gather x1, local copies, waits for them, and re-layouts, on_device(): emit_rows = jnp.take(emission, tokens, axis=0).astype(jnp.float32)  3.35 us
    reduce_sum x1, other arithmetic, absorb_block(): block_total = jnp.sum(shifted, axis=2)  2.81 us
  transfers between devices with their start and end apart: 1, of which 1 were waited for; matrix products, arithmetic and copies ran while one was open for 2% of the time, Pallas kernels for 0%

profile of v1, /device:TPU:0, one launch (start us, length us, event | category | flops | bytes accessed | tf_op | source)
XLA Modules:
  0.0 138.8 jit_solution(12344336109398088085)
XLA Ops:
  7.2 0.0 copy-start
  7.2 0.0 all-gather.2.cloned.1.call-start
  7.2 11.9 %all_gather.12 = bf16[256,1024]{1,0:T(8,128)(2,1)S(1)} all-gather(bf16[256,128]{1,0:T(8,128)(2,1)} %param.8), channel_id=1, replica_groups=mesh['row'=8,'col'=4] {'row'}, dimensions={1}, use_global_device_ids=true | all-gather | bytes 589824 | tf_op jit(solution)/shard_map/all_gather | solution.py:52
  19.1 0.0 copy-done
  19.1 0.4 fusion.11
  19.5 1.8 %copy.19 = f32[64,8,8,128]{3,2,1,0:T(8,128)} copy(f32[64,8,8,128]{3,1,2,0:T(8,128)S(1)} %bitcast.22) | data formatting | bytes 4194304
  21.4 2.2 %reduce_max.19 = f32[512,8]{1,0:T(8,128)S(1)} reduce(f32[512,8,128]{2,1,0:T(8,128)} %bitcast.23, f32[]{:T(128)} %constant.29.clone.1), dimensions={2}, to_apply=%region_0.1 | reduce | flops 520192 | bytes 2113540 | tf_op jit(solution)/shard_map/while/body/eval_jaxpr/reduce_max | solution.py:20
  23.6 2.8 %exponential_reduce_fusion = f32[512,8]{1,0:T(8,128)S(1)} fusion(f32[512,8,128]{2,1,0:T(8,128)} %bitcast.24, f32[512,8]{1,0:T(8,128)S(1)} %reduce_max.19), kind=kLoop, calls=%fused_computation.4 | loop fusion | flops 1044480 | bytes 2129920 | tf_op jit(solution)/shard_map/while/body/eval_jaxpr/reduce_sum | solution.py:22
  26.4 0.1 copy.15
  26.5 0.6 sub.38
  27.1 0.0 copy-start.1
  27.1 1.5 %fusion.9 = (f32[512]{0:T(512)S(1)}, bf16[64,8,8,128]{3,2,1,0:T(8,128)(2,1)}) fusion(f32[512,1024]{1,0:T(8,128)S(1)} %fusion.11, f32[64,8,8,128]{3,2,1,0:T(8,128)S(1)} %bitcast.25), kind=kLoop, calls=%fused_computation.23 | loop fusion | flops 1572352 | bytes 5244928 | tf_op jit(solution)/shard_map/reduce_max | solution.py:57
  28.6 0.0 copy-start.2
  28.6 12.1 %pmax.7 = f32[512]{0:T(512)S(1)} all-reduce(f32[512]{0:T(512)S(1)} %get-tuple-element.29), channel_id=1, replica_groups=mesh['row'=8,'col'=4] {'col'}, use_global_device_ids=true, to_apply=%region_2.3 | all-reduce | flops 512 | bytes 4096 | tf_op jit(solution)/shard_map/pmax | solution.py:59
  40.7 0.2 multiply_reduce_fusion
  41.0 8.4 %psum.14 = f32[512]{0:T(512)S(1)} all-reduce(f32[512]{0:T(512)S(1)} %exponential_multiply_fusion), channel_id=1, replica_groups=mesh['row'=8,'col'=4] {'col'}, use_global_device_ids=true, to_apply=%region_5.0 | all-reduce | flops 512 | bytes 4096 | tf_op jit(solution)/shard_map/psum | solution.py:60
  49.4 0.0 copy-done.1
  49.4 1.6 %convolution_bitcast_fusion = f32[48,8,128]{2,0,1:T(8,128)S(1)} fusion(bf16[64,8,8,128]{3,2,1,0:T(8,128)(2,1)} %get-tuple-element.30, f32[48,512]{1,0:T(8,128)S(1)} %copy-done.1, f32[8,512]{1,0:T(8,128)S(1)} %divide_bitcast_fusion), kind=kOutput, calls=%fused_computation.5 | convolution fusion | flops 50724864 | bytes 1359872 | tf_op jit(solution)/shard_map/while/body/eval_jaxpr/gbi,igk->bgk/dot_general | solution.py:72
  51.0 0.1 copy.17
  51.1 0.7 all_gather.13
  51.8 0.0 all-gather.2.cloned.1.call-update
  51.8 0.0 copy-done.2
  51.8 3.3 %gather_fusion = bf16[48,128]{1,0:T(8,128)(2,1)S(1)} fusion(bf16[16640,128]{1,0:T(8,128)(2,1)} %param.9, s32[1024]{0:T(1024)S(1)} %pad_clamp_fusion), kind=kCustom, calls=%fused_computation | custom fusion | bytes 24768 | tf_op jit(solution)/shard_map/jit(_take)/gather | solution.py:86
  55.2 21.1 %all-gather.2.cloned.1.call-done = f32[8,48,1024]{2,1,0:T(8,128)} async-done(((f32[1,48,1024]{2,1,0:T(8,128)}), f32[8,48,1024]{2,1,0:T(8,128)}) %all-gather.2.cloned.1.call-update) | async-done | bytes 1572880 | tf_op jit(solution)/shard_map/all_gather | solution.py:83
  76.3 1.5 %reduce_sum.39 = f32[48,1024]{1,0:T(8,128)S(1)} reduce(f32[8,48,1024]{2,1,0:T(8,128)} %all-gather.2.cloned.1.call-done, f32[]{:T(128)} %constant.35.clone.1), dimensions={0}, to_apply=%region_6.0 | reduce | flops 344064 | bytes 1769476 | tf_op jit(solution)/shard_map/reduce_sum | solution.py:84
  77.9 0.2 fusion.8
  78.0 39.3 %psum.15 = f32[48]{0:T(128)S(1)} all-reduce(f32[48]{0:T(128)S(1)} %fusion.8), channel_id=1, replica_groups=mesh['row'=8,'col'=4] {'row','col'}, use_global_device_ids=true, to_apply=%region_8.0 | all-reduce | flops 48 | bytes 384 | tf_op jit(solution)/shard_map/psum | solution.py:89
  117.4 0.5 fusion.10
  117.9 0.1 fusion.7
  118.0 13.3 %all_gather.15 = f32[48,512]{1,0:T(8,128)S(1)} all-gather(f32[48,128]{1,0:T(8,128)S(1)} %fusion.7), channel_id=1, replica_groups=mesh['row'=8,'col'=4] {'col'}, dimensions={1}, use_global_device_ids=true | all-gather | bytes 122880 | tf_op jit(solution)/shard_map/all_gather | solution.py:91
  131.3 0.6 copy.29
  (5 shorter events, 0.0 us)
Async XLA Ops:
  7.2 11.9 %copy-start = (bf16[512,256]{1,0:T(8,128)(2,1)S(1)}, bf16[512,256]{1,0:T(8,128)(2,1)}, u32[]{:S(2)}) copy-start(bf16[512,256]{1,0:T(8,128)(2,1)} %param.7) | copy-start | bytes 786436
  7.2 69.2 %all-gather.2.cloned.1.call-start = ((), (), s32[]{:S(2)}) async-start(), calls=%async_computation | async-start | bytes 1769472 | tf_op jit(solution)/shard_map/all_gather | solution.py:83
  27.1 22.3 %copy-start.1 = (f32[48,512]{1,0:T(8,128)S(1)}, f32[48,512]{1,0:T(8,128)}, u32[]{:S(2)}) copy-start(f32[48,512]{1,0:T(8,128)} %param.5) | copy-start | bytes 294916
  28.6 23.2 %copy-start.2 = (s32[48]{0:T(128)S(1)}, s32[48]{0:T(128)}, u32[]{:S(2)}) copy-start(s32[48]{0:T(128)} %param.6) | copy-start | bytes 580
Sparse Core Ops, SparseCore 0:
  51.9 24.3 all-gather.1
